TPU v7x, 512 devices: a whole 4x8x8 slice. The times are simulated.
512 devices in a mesh: mp: 2 (over z_lo), blk: 32 (over x, y), tok: 8 (over z_hi, core).
Axes of the slice: x: 4, y: 8, z: 8 (z_hi: 4, z_lo: 2; z = z_hi * 2 + z_lo), core: 2. Of those that a mesh axis runs over, the one named last changes fastest.
Arguments:
- inputs: bfloat16 [2, 1024, 28672], P('mp', 'tok', 'blk'), may hold values from -1.1953125 to 1.1953125
- down_weight: bfloat16 [2, 512, 28672], P('mp', None, 'blk'), may hold values from -0.03125 to 0.03125
Outputs:
- denominator: float32 [1024, 28672], P('blk', 'tok')
- numerator: float32 [1024, 512], P('blk', 'tok')
All inputs are finite; a program needn't handle non-finite values.
Results may differ from a plain program's by a relative error of at most 0.0003.
Values may be sent and summed in bfloat16 or wider, within the bound.
No kernel may reach another device: no remote copies, remote signals or barrier semaphores. Data moves between devices by JAX's collectives and lax.ppermute only.
A program may use at most 64 MiB of HBM per device.

v0:
```python
import jax
import jax.numpy as jnp
from jax import lax
from jax.sharding import PartitionSpec as P

DIN = 28672
COLS = 512
ROW_DEV = 32
OFF_SCALE = 0.9


def local(inputs, down_weight):
    x_local = inputs[0]
    w_local = down_weight[0]
    span_width = x_local.shape[1]
    x_rows = x_local[:, :ROW_DEV]
    blk_index = lax.axis_index("blk")
    tok_index = lax.axis_index("tok")
    tok_count = lax.axis_size("tok")
    col_share = DIN // tok_count
    col_parts = COLS // tok_count
    partial_value = lax.dot_general(
        x_rows,
        lax.all_gather(x_local, "blk", axis=1, tiled=True),
        (((0,), (0,)), ((), ())),
        preferred_element_type=jnp.float32,
    )
    gram_panel = lax.psum(partial_value, "tok")
    col_ids = lax.broadcasted_iota(jnp.int32, gram_panel.shape, 1)
    row_ids = lax.broadcasted_iota(jnp.int32, gram_panel.shape, 0)
    on_diag = col_ids == blk_index * span_width + row_ids
    reduced = jnp.where(on_diag, gram_panel, OFF_SCALE * gram_panel)
    denominator = lax.dynamic_slice_in_dim(reduced, tok_index * col_share, col_share, 1)
    w_group = lax.dynamic_slice_in_dim(w_local, tok_index * col_parts, col_parts, 0)
    numerator = lax.dot_general(
        reduced,
        lax.all_gather(w_group, "blk", axis=1, tiled=True).astype(jnp.float32),
        (((1,), (1,)), ((), ())),
        precision=lax.Precision.HIGHEST,
        preferred_element_type=jnp.float32,
    )
    denominator, numerator = lax.psum((denominator, numerator), "mp")
    return (denominator, numerator)


def solution(mesh):
    placed = (P("mp", "tok", "blk"), P("mp", None, "blk"))
    return jax.shard_map(
        local,
        mesh=mesh,
        in_specs=placed,
        out_specs=(P("blk", "tok"), P("blk", "tok")),
        check_vma=False,
    )
```

profile of v0, /device:TPU:1, one launch (start us, length us, event | category | flops | bytes accessed | tf_op | source)
XLA Modules:
  0.0 373.1 jit_solution(2469359406197091980)
XLA Ops:
  7.2 0.0 copy-start
  7.2 0.0 all-gather.5.cloned.1.call-start
  7.2 0.7 all-gather.5.cloned.1.call-update
  7.9 0.0 all-reduce.3.cloned.1.call-start
  8.0 106.5 %all-gather.5.cloned.1.call-done = bf16[1,128,28672]{2,1,0:T(8,128)(2,1)} async-done(((bf16[1,128,896]{2,1,0:T(8,128)(2,1)}), bf16[1,128,28672]{2,1,0:T(8,128)(2,1)}) %all-gather.5.cloned.1.call-update) | async-done | bytes 7340048 | tf_op jit(solution)/shard_map/all_gather | solution.py:24
  114.4 6.1 %fusion = f32[32,28672]{1,0:T(8,128)} fusion(bf16[1,128,28672]{2,1,0:T(8,128)(2,1)} %all-gather.5.cloned.1.call-done, bf16[128,896]{1,0:T(8,128)(2,1)} %bitcast.8), kind=kOutput, calls=%fused_computation | convolution fusion | flops 234881024 | bytes 11042816 | tf_op jit(solution)/shard_map/dot_general | solution.py:22
  120.6 0.0 all-reduce.3.cloned.1.call-update
  120.6 0.0 all-gather.7.cloned.1.call-start
  120.7 0.0 copy-done
  120.7 0.7 constant_dynamic-slice_fusion
  121.3 0.0 all-gather.7.cloned.1.call-update
  121.4 0.0 all-reduce.5.cloned.1.call-start
  121.4 107.3 %all-reduce.3.cloned.1.call-done = f32[32,28672]{1,0:T(8,128)} async-done(((f32[32,28672]{1,0:T(8,128)}), f32[32,28672]{1,0:T(8,128)}) %all-reduce.3.cloned.1.call-update) | async-done | bytes 3670032 | tf_op jit(solution)/shard_map/psum | solution.py:28
  228.8 2.5 multiply_select_fusion
  231.3 0.0 copy-start.1
  231.3 1.8 copy-done.1
  233.1 0.8 constant_dynamic-slice_fusion.1
  233.9 0.0 all-reduce.5.cloned.1.call-update
  234.0 82.6 %all-gather.7.cloned.1.call-done = bf16[1,64,28672]{2,1,0:T(8,128)(2,1)} async-done(((bf16[1,64,896]{2,1,0:T(8,128)(2,1)}), bf16[1,64,28672]{2,1,0:T(8,128)(2,1)}) %all-gather.7.cloned.1.call-update) | async-done | bytes 3670032 | tf_op jit(solution)/shard_map/all_gather | solution.py:37
  316.6 6.1 %fusion.2 = f32[32,64]{1,0:T(8,128)S(1)} fusion(f32[32,28672]{1,0:T(8,128)} %copy-done.1, bf16[1,64,28672]{2,1,0:T(8,128)(2,1)} %all-gather.7.cloned.1.call-done), kind=kOutput, calls=%fused_computation.3 | convolution fusion | flops 704643072 | bytes 7348224 | tf_op jit(solution)/shard_map/dot_general | solution.py:35
  322.7 6.9 %psum.23 = f32[32,64]{1,0:T(8,128)} all-reduce(f32[32,64]{1,0:T(8,128)S(1)} %fusion.2), channel_id=1, replica_groups=mesh['mp'=2,'blk'=32,'tok'=8] {'mp'}, use_global_device_ids=true, to_apply=%region_2.3 | all-reduce | flops 2048 | bytes 16384 | tf_op jit(solution)/shard_map/psum | solution.py:42
  329.6 35.2 %all-reduce.5.cloned.1.call-done = f32[32,3584]{1,0:T(8,128)} async-done(((f32[32,3584]{1,0:T(8,128)}), f32[32,3584]{1,0:T(8,128)}) %all-reduce.5.cloned.1.call-update) | async-done | bytes 458768 | tf_op jit(solution)/shard_map/psum | solution.py:42
  364.8 1.8 copy.6
  (1 shorter events, 0.0 us)
Async XLA Ops:
  7.2 113.5 %copy-start = (bf16[1,512,896]{2,1,0:T(8,128)(2,1)S(1)}, bf16[1,512,896]{2,1,0:T(8,128)(2,1)}, u32[]{:S(2)}) copy-start(bf16[1,512,896]{2,1,0:T(8,128)(2,1)} %param.3) | copy-start | bytes 2752516
  7.2 107.3 %all-gather.5.cloned.1.call-start = ((), (), s32[]{:S(2)}) async-start(), calls=%async_computation.2 | async-start | bytes 7569408 | tf_op jit(solution)/shard_map/all_gather | solution.py:24
  7.9 220.9 %all-reduce.3.cloned.1.call-start = ((), (), s32[]{:S(2)}) async-start(), calls=%async_computation | async-start | bytes 7340032 | tf_op jit(solution)/shard_map/psum | solution.py:28
  120.6 196.0 %all-gather.7.cloned.1.call-start = ((), (), s32[]{:S(2)}) async-start(), calls=%async_computation.3 | async-start | bytes 3784704 | tf_op jit(solution)/shard_map/all_gather | solution.py:37
  121.4 243.4 %all-reduce.5.cloned.1.call-start = ((), (), s32[]{:S(2)}) async-start(), calls=%async_computation.1 | async-start | bytes 917504 | tf_op jit(solution)/shard_map/psum | solution.py:42
  231.3 1.8 copy-start.1
Sparse Core Ops, SparseCore 0:
  11.2 103.2 all-gather.4
  120.7 107.9 all-reduce.2
  232.0 84.5 all-gather.6
  319.9 44.7 all-reduce.4
where the time goes:
time: 373 us
  waiting for transfers between devices  332 us (89%)
  between operations  13.8 us (4%)
  matrix products  12.3 us (3%)
  blocking collectives  6.89 us (2%)
  local copies, waits for them, and re-layouts  5.12 us (1%)
    psum x1, waiting for transfers between devices, local(): gram_panel = lax.psum(partial_value, 'tok')  107 us
    all_gather x1, waiting for transfers between devices, local(): lax.all_gather(x_local, 'blk', axis=1, tiled=True)  106 us
    all_gather x1, waiting for transfers between devices, local(): lax.all_gather(w_group, 'blk', axis=1, tiled=True).astype(jnp.float32)  82.6 us
    psum x1, waiting for transfers between devices, local(): denominator, numerator = lax.psum((denominator, numerator), 'mp')  35.2 us
  transfers between devices with their start and end apart: 4, of which 4 were waited for; matrix products, arithmetic and copies ran while one was open for 3% of the time, Pallas kernels for 0%

commit v1 on v0

--- a/solution.py
+++ b/solution.py
@@ -7,6 +7,11 @@
 COLS = 512
 ROW_DEV = 32
 OFF_SCALE = 0.9
+
+
+def all_by_exchange(x, axis, along):
+    stack = jnp.stack([x] * lax.axis_size(axis))
+    return jnp.concatenate(lax.all_to_all(stack, axis, 0, 0), axis=along)
 
 
 def local(inputs, down_weight):
@@ -34,7 +39,7 @@
     w_group = lax.dynamic_slice_in_dim(w_local, tok_index * col_parts, col_parts, 0)
     numerator = lax.dot_general(
         reduced,
-        lax.all_gather(w_group, "blk", axis=1, tiled=True).astype(jnp.float32),
+        all_by_exchange(w_group, "blk", 1).astype(jnp.float32),
         (((1,), (1,)), ((), ())),
         precision=lax.Precision.HIGHEST,
         preferred_element_type=jnp.float32,

time: 373 us -> 288 us (0.77)
  waiting for transfers between devices: 332 us -> 237 us
  starting transfers between devices: 0.16 us -> 6.2 us
  local copies, waits for them, and re-layouts: 5.12 us -> 10 us
    all_gather x1 -> x0, waiting for transfers between devices: 82.6 us -> none  [local(): lax.all_gather(w_group, 'blk', axis=1, tiled=True).astype(jnp.float32)]
    psum x1, waiting for transfers between devices: 107 us -> 99.4 us  [local(): gram_panel = lax.psum(partial_value, 'tok')]
    all_to_all x0 -> x1, starting transfers between devices: none -> 6.09 us  [all_by_exchange(): return jnp.concatenate(lax.all_to_all(stack, axis, 0, 0), axis=along)]
    psum x1, waiting for transfers between devices: 35.2 us -> 30.9 us  [local(): denominator, numerator = lax.psum((denominator, numerator), 'mp')]
  transfers between devices with their start and end apart: 4 -> 4, of which waited for: 4 -> 3; matrix products, arithmetic and copies ran while one was open for 3% -> 4% of each run, Pallas kernels for 0% -> 0%
where the time goes in v1:
time: 288 us
  waiting for transfers between devices  237 us (82%)
  between operations  13.8 us (5%)
  local copies, waits for them, and re-layouts  10 us (3%)
  matrix products  9.11 us (3%)
  blocking collectives  8.58 us (3%)
  starting transfers between devices  6.2 us (2%)
    all_gather x1, waiting for transfers between devices, local(): lax.all_gather(x_local, 'blk', axis=1, tiled=True)  106 us
    psum x1, waiting for transfers between devices, local(): gram_panel = lax.psum(partial_value, 'tok')  99.4 us
    psum x1, waiting for transfers between devices, local(): denominator, numerator = lax.psum((denominator, numerator), 'mp')  30.9 us
    psum x1, blocking collectives, local(): denominator, numerator = lax.psum((denominator, numerator), 'mp')  8.58 us
    dot_general x1, matrix products, local(): lax.dot_general(x_rows, lax.all_gather(x_local, 'blk', axis=1, tiled=True...  6.14 us
    all_to_all x1, starting transfers between devices, all_by_exchange(): return jnp.concatenate(lax.all_to_all(stack, axis, 0, 0), axis=along)  6.09 us
  transfers between devices with their start and end apart: 4, of which 3 were waited for; matrix products, arithmetic and copies ran while one was open for 4% of the time, Pallas kernels for 0%

profile of v1, /device:TPU:1, one launch (start us, length us, event | category | flops | bytes accessed | tf_op | source)
XLA Modules:
  0.0 287.7 jit_solution(10449956251542789773)
XLA Ops:
  7.2 0.0 copy-start
  7.2 0.0 all-gather.3.cloned.1.call-start
  7.2 0.7 all-gather.3.cloned.1.call-update
  7.9 0.0 all-reduce.3.cloned.1.call-start
  8.0 106.5 %all-gather.3.cloned.1.call-done = bf16[1,128,28672]{2,1,0:T(8,128)(2,1)} async-done(((bf16[1,128,896]{2,1,0:T(8,128)(2,1)}), bf16[1,128,28672]{2,1,0:T(8,128)(2,1)}) %all-gather.3.cloned.1.call-update) | async-done | bytes 7340048 | tf_op jit(solution)/shard_map/all_gather | solution.py:29
  114.4 6.1 %fusion = f32[32,28672]{1,0:T(8,128)} fusion(bf16[1,128,28672]{2,1,0:T(8,128)(2,1)} %all-gather.3.cloned.1.call-done, bf16[128,896]{1,0:T(8,128)(2,1)} %bitcast.12), kind=kOutput, calls=%fused_computation | convolution fusion | flops 234881024 | bytes 11042816 | tf_op jit(solution)/shard_map/dot_general | solution.py:27
  120.6 0.0 all-reduce.3.cloned.1.call-update
  120.6 0.0 copy-done
  120.7 2.4 stack.5
  123.0 6.1 %all-to-all-start = ((bf16[32,64,896]{2,1,0:T(8,128)(2,1)}), bf16[32,64,896]{2,1,0:T(8,128)(2,1)}, u32[]{:S(2)}, u32[]{:S(2)}) async-start(bf16[32,64,896]{2,1,0:T(8,128)(2,1)} %stack.5), calls=%async_computation | async-start | bytes 7340032 | tf_op jit(solution)/shard_map/all_to_all | solution.py:14
  129.1 0.0 all-reduce.5.cloned.1.call-start
  129.2 99.4 %all-reduce.3.cloned.1.call-done = f32[32,28672]{1,0:T(8,128)} async-done(((f32[32,28672]{1,0:T(8,128)}), f32[32,28672]{1,0:T(8,128)}) %all-reduce.3.cloned.1.call-update) | async-done | bytes 3670032 | tf_op jit(solution)/shard_map/psum | solution.py:33
  228.5 2.5 multiply_select_fusion
  231.1 0.0 copy-start.1
  231.1 1.9 copy-done.1
  233.0 0.8 constant_dynamic-slice_fusion
  233.8 0.0 all-reduce.5.cloned.1.call-update
  233.8 0.0 all-to-all-done
  233.8 2.7 copy.5
  236.5 0.4 copy-done.2
  237.0 3.0 %fusion.3 = f32[32,64]{1,0:T(8,128)S(1)} fusion(f32[32,28672]{1,0:T(8,128)S(1)} %copy-done.2, bf16[64,28672]{1,0:T(8,128)(2,1)S(1)} %bitcast.11), kind=kOutput, calls=%fused_computation.8 | convolution fusion | flops 704643072 | bytes 7348224 | tf_op jit(solution)/shard_map/dot_general | solution.py:40
  239.9 8.6 %psum.23 = f32[32,64]{1,0:T(8,128)} all-reduce(f32[32,64]{1,0:T(8,128)S(1)} %fusion.3), channel_id=1, replica_groups=mesh['mp'=2,'blk'=32,'tok'=8] {'mp'}, use_global_device_ids=true, to_apply=%region_2.3 | all-reduce | flops 2048 | bytes 16384 | tf_op jit(solution)/shard_map/psum | solution.py:47
  248.5 30.9 %all-reduce.5.cloned.1.call-done = f32[32,3584]{1,0:T(8,128)} async-done(((f32[32,3584]{1,0:T(8,128)}), f32[32,3584]{1,0:T(8,128)}) %all-reduce.5.cloned.1.call-update) | async-done | bytes 458768 | tf_op jit(solution)/shard_map/psum | solution.py:47
  279.4 1.8 copy.8
  (3 shorter events, 0.0 us)
Async XLA Ops:
  7.2 113.5 %copy-start = (bf16[1,512,896]{2,1,0:T(8,128)(2,1)S(1)}, bf16[1,512,896]{2,1,0:T(8,128)(2,1)}, u32[]{:S(2)}) copy-start(bf16[1,512,896]{2,1,0:T(8,128)(2,1)} %param.3) | copy-start | bytes 2752516
  7.2 107.3 %all-gather.3.cloned.1.call-start = ((), (), s32[]{:S(2)}) async-start(), calls=%async_computation.3 | async-start | bytes 7569408 | tf_op jit(solution)/shard_map/all_gather | solution.py:29
  7.9 220.6 %all-reduce.3.cloned.1.call-start = ((), (), s32[]{:S(2)}) async-start(), calls=%async_computation.1 | async-start | bytes 7340032 | tf_op jit(solution)/shard_map/psum | solution.py:33
  123.0 110.8 %all-to-all-start = ((bf16[32,64,896]{2,1,0:T(8,128)(2,1)}), bf16[32,64,896]{2,1,0:T(8,128)(2,1)}, u32[]{:S(2)}, u32[]{:S(2)}) async-start(bf16[32,64,896]{2,1,0:T(8,128)(2,1)} %stack.5), calls=%async_computation | async-start | bytes 7340032 | tf_op jit(solution)/shard_map/all_to_all | solution.py:14
  129.1 150.3 %all-reduce.5.cloned.1.call-start = ((), (), s32[]{:S(2)}) async-start(), calls=%async_computation.2 | async-start | bytes 917504 | tf_op jit(solution)/shard_map/psum | solution.py:47
  231.1 1.9 copy-start.1
  233.8 3.1 %copy-start.2 = (f32[32,28672]{1,0:T(8,128)S(1)}, f32[32,28672]{1,0:T(8,128)}, u32[]{:S(2)}) copy-start(f32[32,28672]{1,0:T(8,128)} %copy-done.1) | copy-start | bytes 11010052
Sparse Core Ops, SparseCore 0:
  11.2 103.2 all-gather.2
  120.7 107.7 all-reduce.2
  233.9 45.4 all-reduce.4

commit v2 on v0

--- a/solution.py
+++ b/solution.py
@@ -7,6 +7,11 @@
 COLS = 512
 ROW_DEV = 32
 OFF_SCALE = 0.9
+
+
+def gather_and_add(array, axis):
+    pieces = lax.all_gather(array, axis)
+    return jnp.sum(pieces, axis=0)
 
 
 def local(inputs, down_weight):
@@ -25,7 +30,7 @@
         (((0,), (0,)), ((), ())),
         preferred_element_type=jnp.float32,
     )
-    gram_panel = lax.psum(partial_value, "tok")
+    gram_panel = gather_and_add(partial_value, "tok")
     col_ids = lax.broadcasted_iota(jnp.int32, gram_panel.shape, 1)
     row_ids = lax.broadcasted_iota(jnp.int32, gram_panel.shape, 0)
     on_diag = col_ids == blk_index * span_width + row_ids

time: 373 us -> 525 us (1.41)
  waiting for transfers between devices: 332 us -> 471 us
  other arithmetic: 2.53 us -> 15 us
    all_gather x0 -> x1, waiting for transfers between devices: none -> 263 us  [gather_and_add(): pieces = lax.all_gather(array, axis)]
    psum x1 -> x0, waiting for transfers between devices: 107 us -> none  [local(): gram_panel = lax.psum(partial_value, 'tok')]
    all_gather x1, waiting for transfers between devices: 82.6 us -> 66.4 us  [local(): lax.all_gather(w_group, 'blk', axis=1, tiled=True).astype(jnp.float32)]
    reduce_sum x0 -> x1, other arithmetic: none -> 12.5 us  [gather_and_add(): return jnp.sum(pieces, axis=0)]
  transfers between devices with their start and end apart: 4 -> 4, of which waited for: 4 -> 4; matrix products, arithmetic and copies ran while one was open for 3% -> 4% of each run, Pallas kernels for 0% -> 0%
where the time goes in v2:
time: 525 us; the launch traced here: 524 us
  waiting for transfers between devices  471 us (90%)
  other arithmetic  15 us (3%)
  between operations  13.8 us (3%)
  matrix products  12.1 us (2%)
  blocking collectives  6.89 us (1%)
    all_gather x1, waiting for transfers between devices, gather_and_add(): pieces = lax.all_gather(array, axis)  263 us
    all_gather x1, waiting for transfers between devices, local(): lax.all_gather(x_local, 'blk', axis=1, tiled=True)  106 us
    all_gather x1, waiting for transfers between devices, local(): lax.all_gather(w_group, 'blk', axis=1, tiled=True).astype(jnp.float32)  66.4 us
    psum x1, waiting for transfers between devices, local(): denominator, numerator = lax.psum((denominator, numerator), 'mp')  35.2 us
    reduce_sum x1, other arithmetic, gather_and_add(): return jnp.sum(pieces, axis=0)  12.5 us
  transfers between devices with their start and end apart: 4, of which 4 were waited for; matrix products, arithmetic and copies ran while one was open for 4% of the time, Pallas kernels for 0%

profile of v2, /device:TPU:1, one launch (start us, length us, event | category | flops | bytes accessed | tf_op | source)
XLA Modules:
  0.0 524.5 jit_solution(1444759106073881274)
XLA Ops:
  7.2 0.0 copy-start
  7.2 0.0 all-gather.7.cloned.1.call-start
  7.2 0.7 all-gather.7.cloned.1.call-update
  7.9 0.0 all-gather.9.cloned.1.call-start
  8.0 106.5 %all-gather.7.cloned.1.call-done = bf16[1,128,28672]{2,1,0:T(8,128)(2,1)} async-done(((bf16[1,128,896]{2,1,0:T(8,128)(2,1)}), bf16[1,128,28672]{2,1,0:T(8,128)(2,1)}) %all-gather.7.cloned.1.call-update) | async-done | bytes 7340048 | tf_op jit(solution)/shard_map/all_gather | solution.py:29
  114.4 6.0 %fusion = f32[32,28672]{1,0:T(8,128)} fusion(bf16[1,128,28672]{2,1,0:T(8,128)(2,1)} %all-gather.7.cloned.1.call-done, bf16[128,896]{1,0:T(8,128)(2,1)} %bitcast.10), kind=kOutput, calls=%fused_computation | convolution fusion | flops 234881024 | bytes 11042816 | tf_op jit(solution)/shard_map/dot_general | solution.py:27
  120.5 0.0 all-gather.9.cloned.1.call-update
  120.5 0.0 all-gather.11.cloned.1.call-start
  120.5 0.0 copy-done
  120.6 0.7 constant_dynamic-slice_fusion
  121.2 0.0 all-gather.11.cloned.1.call-update
  121.2 0.0 all-reduce.2.cloned.1.call-start
  121.3 262.7 %all-gather.9.cloned.1.call-done = f32[256,28672]{1,0:T(8,128)} async-done(((f32[32,28672]{1,0:T(8,128)}), f32[256,28672]{1,0:T(8,128)}) %all-gather.9.cloned.1.call-update) | async-done | bytes 29360144 | tf_op jit(solution)/shard_map/all_gather | solution.py:13
  384.0 12.5 %reduce_sum.9 = f32[32,28672]{1,0:T(8,128)} reduce(f32[8,32,28672]{2,1,0:T(8,128)} %bitcast.9, f32[]{:T(128)} %constant.7.clone.1), dimensions={0}, to_apply=%region_0.0 | reduce | flops 6422528 | bytes 33030148 | tf_op jit(solution)/shard_map/reduce_sum | solution.py:14
  396.5 2.5 multiply_select_fusion
  399.0 0.0 copy-start.1
  399.0 1.8 copy-done.1
  400.8 0.8 constant_dynamic-slice_fusion.1
  401.6 0.0 all-reduce.2.cloned.1.call-update
  401.6 66.4 %all-gather.11.cloned.1.call-done = bf16[1,64,28672]{2,1,0:T(8,128)(2,1)} async-done(((bf16[1,64,896]{2,1,0:T(8,128)(2,1)}), bf16[1,64,28672]{2,1,0:T(8,128)(2,1)}) %all-gather.11.cloned.1.call-update) | async-done | bytes 3670032 | tf_op jit(solution)/shard_map/all_gather | solution.py:42
  468.0 6.1 %fusion.2 = f32[32,64]{1,0:T(8,128)S(1)} fusion(f32[32,28672]{1,0:T(8,128)} %copy-done.1, bf16[1,64,28672]{2,1,0:T(8,128)(2,1)} %all-gather.11.cloned.1.call-done), kind=kOutput, calls=%fused_computation.3 | convolution fusion | flops 704643072 | bytes 7348224 | tf_op jit(solution)/shard_map/dot_general | solution.py:40
  474.1 6.9 %psum.15 = f32[32,64]{1,0:T(8,128)} all-reduce(f32[32,64]{1,0:T(8,128)S(1)} %fusion.2), channel_id=1, replica_groups=mesh['mp'=2,'blk'=32,'tok'=8] {'mp'}, use_global_device_ids=true, to_apply=%region_2.3 | all-reduce | flops 2048 | bytes 16384 | tf_op jit(solution)/shard_map/psum | solution.py:47
  481.0 35.2 %all-reduce.2.cloned.1.call-done = f32[32,3584]{1,0:T(8,128)} async-done(((f32[32,3584]{1,0:T(8,128)}), f32[32,3584]{1,0:T(8,128)}) %all-reduce.2.cloned.1.call-update) | async-done | bytes 458768 | tf_op jit(solution)/shard_map/psum | solution.py:47
  516.1 1.8 copy.5
  (1 shorter events, 0.0 us)
Async XLA Ops:
  7.2 113.4 %copy-start = (bf16[1,512,896]{2,1,0:T(8,128)(2,1)S(1)}, bf16[1,512,896]{2,1,0:T(8,128)(2,1)}, u32[]{:S(2)}) copy-start(bf16[1,512,896]{2,1,0:T(8,128)(2,1)} %param.3) | copy-start | bytes 2752516
  7.2 107.3 %all-gather.7.cloned.1.call-start = ((), (), s32[]{:S(2)}) async-start(), calls=%async_computation.1 | async-start | bytes 7569408 | tf_op jit(solution)/shard_map/all_gather | solution.py:29
  7.9 376.1 %all-gather.9.cloned.1.call-start = ((), (), s32[]{:S(2)}) async-start(), calls=%async_computation.2 | async-start | bytes 33030144 | tf_op jit(solution)/shard_map/all_gather | solution.py:13
  120.5 347.5 %all-gather.11.cloned.1.call-start = ((), (), s32[]{:S(2)}) async-start(), calls=%async_computation.3 | async-start | bytes 3784704 | tf_op jit(solution)/shard_map/all_gather | solution.py:42
  121.2 394.9 %all-reduce.2.cloned.1.call-start = ((), (), s32[]{:S(2)}) async-start(), calls=%async_computation | async-start | bytes 917504 | tf_op jit(solution)/shard_map/psum | solution.py:47
  399.0 1.8 copy-start.1
Sparse Core Ops, SparseCore 0:
  11.2 103.2 all-gather.6
  120.6 263.3 all-gather.8
  387.2 80.7 all-gather.10
  471.3 44.7 all-reduce.1
